TPU v7x, 32 devices: a whole 2x2x4 slice. The times are simulated.
32 devices in a mesh: slab: 8 (over y, x, core), energy: 4 (over z).
Axes of the slice: x: 2, y: 2, z: 4, core: 2. Of those that a mesh axis runs over, the one named last changes fastest.
Arguments:
- onsite: float32 [8, 256, 256], P('slab'), may hold values from -1.4 to 0.3, as said below
- coupling: float32 [8, 256, 256], P('slab'), may hold values from -0.25 to 1.6
- pattern: int32 [8, 4, 4], P('slab'), may hold values 0 or 1
- contact_rates: float32 [2, 256], replicated, may hold values from 1 to 3
- energy_index: int32 [16], P('energy'), parts along dimension 0, may hold values from 0 to 31
Outputs:
- spectral: float32 [8, 16, 256], P('slab', 'energy'), parts along dimension 1
- transmission: float32 [16], P('energy'), parts along dimension 0
There are 4 independent parts, one for each index of `energy`. A program takes and returns all parts, laid end to end along the dimension named above; an argument that names none is the same for every part. Nothing has to cross between parts.
Inputs may be any that keep to these rules, and one draw needn't show every extreme that they name: Every onsite block is symmetric.
All inputs are finite; a program needn't handle non-finite values. No bound on the sum of `pattern` on one device may be relied on, other than what follows from the above.
Results may differ from a plain program's by a relative error of at most 0.00012.
Values sent between devices are 32-bit elements; how exact they have to be, the bound alone decides.
A program may use at most 64 MiB of HBM per device.

v0:
```python
import functools

import jax
import jax.numpy as jnp
from jax import lax
from jax.experimental import pallas as pl
from jax.experimental.pallas import tpu as pltpu
from jax.sharding import PartitionSpec as P

energy_floor = -0.2
energy_spacing = 0.0125
broadening = 0.3
MESH = pl.DeviceIdType.MESH
f32, bf16 = jnp.float32, jnp.bfloat16


def split(x):
    high = x.astype(bf16)
    return high, (x - high.astype(f32)).astype(bf16)


def product(left, right):
    return jnp.dot(
        jnp.concatenate([left[0], left[0], left[1]], axis=1),
        jnp.concatenate([right[0], right[1], right[0]], axis=0),
        preferred_element_type=f32,
    )


def complex_product(left, right):
    first = product(left[0], right[0])
    second = product(left[1], right[1])
    third = product(left[2], right[2])
    return first - second, third - first - second


def split3(real, imag):
    return split(real), split(imag), split(real + imag)


def exclusive(index, other, count):
    if count & (count - 1):
        return (index + other) % count
    total, bit = 0, 1
    while bit < count:
        total = total + (((index // bit) + (other // bit) % 2) % 2) * bit
        bit *= 2
    return total


def kernel(
    n, ne, w,
    onsite_in, coupling_in, pattern_ref, rates_ref, index_ref,
    spectral_ref, crossing_ref,
    raw, o_buf, m_buf, hist, other, factor, rows, crossing_own, rows_in, crossing_in,
    local_sem, o_send, m_send, h_send, h_recv, o_fsend, m_fsend, o_recv, m_recv,
    s_send, s_recv, r_send, r_recv, t_send, t_recv,
):
    half = n // 2
    group = 2 * ne
    me = lax.axis_index("slab")
    side = me % 2
    partner = me + 1 - 2 * side
    mine = (me // 2) % ne
    base = (me // group) * group

    def slab_at(t):
        return t + side * (n - 1 - 2 * t)

    def coupling_at(t):
        return t + side * (n - 2 - 2 * t)

    def remote(src, dst, send, recv, target):
        return pltpu.make_async_remote_copy(
            src_ref=src, dst_ref=dst, send_sem=send, recv_sem=recv,
            device_id={"slab": target}, device_id_type=MESH,
        )

    own_o = pltpu.make_async_copy(onsite_in.at[0], raw.at[0], local_sem.at[0])
    own_m = pltpu.make_async_copy(coupling_in.at[0], raw.at[1], local_sem.at[1])
    own_o.start()
    own_m.start()

    barrier = pltpu.get_barrier_semaphore()
    for step in range(1, n):
        pl.semaphore_signal(
            barrier, inc=1, device_id={"slab": (me + step) % n}, device_id_type=MESH
        )

    h = w // 2
    tile_row = lax.broadcasted_iota(jnp.int32, (h, h), 0)
    tile_column = lax.broadcasted_iota(jnp.int32, (h, h), 1)

    def packed(block):
        last = block[h:, h:]
        o_buf[me, :h, :h] = jnp.where(tile_row >= tile_column, block[:h, :h], last)
        o_buf[me, :h, h:] = block[:h, h:]
        diag = jnp.sum(jnp.where(tile_row == tile_column, last, 0.0), axis=0, keepdims=True)
        o_buf[me, h:, :] = jnp.broadcast_to(jnp.concatenate([diag, diag], axis=1), (8, w))

    def unpacked(j):
        both = o_buf[j, :h, :h]
        corner = o_buf[j, :h, h:]
        turned = both.T
        first = jnp.where(tile_row >= tile_column, both, turned)
        last = jnp.where(tile_row < tile_column, both, turned)
        last = jnp.where(tile_row == tile_column, o_buf[j, h : h + 1, :h], last)
        return jnp.concatenate(
            [
                jnp.concatenate([first, corner], axis=1),
                jnp.concatenate([corner.T, last], axis=1),
            ],
            axis=0,
        )

    own_o.wait()
    own_m.wait()
    packed(raw[0])
    tiles = pattern_ref.shape[1]
    size = w // tiles
    lane_tile = lax.broadcasted_iota(jnp.int32, (1, w), 1) // size
    for p in range(tiles):
        kept = jnp.zeros((1, w), f32)
        for q in range(tiles):
            kept = jnp.where(lane_tile == q, pattern_ref[0, p, q].astype(f32), kept)
        m_buf[me, p * size : (p + 1) * size, :] = raw[1, p * size : (p + 1) * size, :] * kept
    pl.semaphore_wait(barrier, n - 1)

    square = half == 4
    chip = me // 2
    if square:
        aside = exclusive(chip, 1, half) * 2 + side
        above = exclusive(chip, 2, half) * 2 + side
        targets = [aside, above]
    else:
        aside = above = me
        targets = [exclusive(chip, k, half) * 2 + side for k in range(half - 1, 0, -1)]
    cut = w // 4
    top, bottom = pl.ds(0, cut), pl.ds(cut, w - cut)

    def o_part(j, k, target):
        return remote(o_buf.at[j], o_buf.at[j], o_send.at[k], o_recv.at[j], target)

    def top_part(j, k, target):
        return remote(
            m_buf.at[j, top], m_buf.at[j, top], h_send.at[k], h_recv.at[j], target
        )

    def bottom_part(j, k, target):
        return remote(
            m_buf.at[j, bottom], m_buf.at[j, bottom], m_send.at[k], m_recv.at[j], target
        )

    def used(j, act):
        pl.when(j < n - 1)(act)

    def send_first(j, k, target):
        o_part(j, k, target).start()
        used(j, lambda: top_part(j, k, target).start())

    def send_second(j, k, target):
        used(j, lambda: bottom_part(j, k, target).start())

    def arrived(buf, sems, j):
        remote(buf.at[j], buf.at[j], o_send.at[0], sems.at[j], partner).wait_recv()

    def direct(j):
        @pl.when((j != me) & (j != aside))
        def _():
            top_part(j, 0, partner).wait_recv()

        @pl.when((j != me) & (j != above))
        def _():
            bottom_part(j, 0, partner).wait_recv()

    if square:
        send_first(me, 0, aside)
        send_second(me, 1, above)
        outer = (chip == 0) | (chip == half - 1)

        def own_rest():
            send_second(me, 0, aside)
            send_first(me, 1, above)

        pl.when(outer)(own_rest)
        o_part(aside, 0, partner).wait_recv()
        o_part(aside, 2, above).start()

        @pl.when(aside < n - 1)
        def _():
            top_part(aside, 0, partner).wait_recv()
            top_part(aside, 2, above).start()

        used(above, lambda: bottom_part(above, 0, partner).wait_recv())
        send_second(above, 2, aside)
        pl.when(jnp.logical_not(outer))(own_rest)
    else:
        for k, target in enumerate(targets):
            send_first(me, k, target)
            send_second(me, k, target)

    def o_forward(j):
        return remote(o_buf.at[j], o_buf.at[j], o_fsend.at[j], o_recv.at[j], partner)

    def m_forward(j):
        return remote(m_buf.at[j], m_buf.at[j], m_fsend.at[j], m_recv.at[j], partner)

    def s_forward(t):
        return remote(hist.at[t], other.at[t], s_send.at[t], s_recv.at[t], partner)

    row_at = lax.broadcasted_iota(jnp.int32, (w, w), 0)
    column_at = lax.broadcasted_iota(jnp.int32, (w, w), 1)
    eye = row_at == column_at
    energy = energy_floor + energy_spacing * index_ref[mine].astype(f32)

    def scaled(real, imag):
        diag_real = jnp.sum(jnp.where(eye, real, 0.0), axis=0, keepdims=True)
        diag_imag = jnp.sum(jnp.where(eye, imag, 0.0), axis=0, keepdims=True)
        modulus = diag_real * diag_real + diag_imag * diag_imag
        xr = diag_real / modulus
        xi = -diag_imag / modulus
        xrc = jnp.sum(jnp.where(eye, xr, 0.0), axis=1, keepdims=True)
        xic = jnp.sum(jnp.where(eye, xi, 0.0), axis=1, keepdims=True)
        off_real = jnp.where(eye, 0.0, real)
        off_imag = jnp.where(eye, 0.0, imag)
        fr = off_real * xr - off_imag * xi
        fi = off_real * xi + off_imag * xr
        return (xr, xi, xrc, xic), (off_real, off_imag), (fr, fi)

    def completed(x, f, f_parts, f2):
        third = complex_product(f_parts, split3(*f2))
        hr = jnp.where(eye, 1.0, 0.0) - f[0] + f2[0] - third[0]
        hi = f2[1] - f[1] - third[1]
        xrc, xic = x[2], x[3]
        return xrc * hr - xic * hi, xrc * hi + xic * hr

    def diagonal(x, off, f, f2):
        xr, xi, xrc, xic = x
        zr = off[0] * xrc - off[1] * xic
        zi = off[0] * xic + off[1] * xrc
        wr = f[0] - f2[0]
        wi = f[1] - f2[1]
        dr = 1.0 + jnp.sum(zr * wr - zi * wi, axis=0, keepdims=True)
        di = jnp.sum(zr * wi + zi * wr, axis=0, keepdims=True)
        return -2.0 * (xr * di + xi * dr)

    def matrix(t, slot):
        own = unpacked(slab_at(t))
        real = jnp.where(eye, energy, 0.0) - own - hist[slot, 0]
        imag = jnp.where(eye, broadening, 0.0) - hist[slot, 1]
        return real, imag

    def chain(t, a, slot):
        m = m_buf[coupling_at(t)]
        high, low = split(m)
        factor[side, 0] = high
        factor[side, 1] = low
        high, low = split(m.T)
        factor[1 - side, 0] = high
        factor[1 - side, 1] = low
        x, off, f = scaled(*a)
        parts = split3(*f)
        f2 = complex_product(parts, parts)
        g = completed(x, f, parts, f2)
        gs = split(jnp.concatenate(g, axis=0))
        u = product(gs, (factor[0, 0], factor[0, 1]))
        us = split(jnp.concatenate([u[:w], u[w:]], axis=1))
        s = product((factor[1, 0], factor[1, 1]), us)
        hist[slot, 0] = s[:, :w]
        hist[slot, 1] = s[:, w:]

    def final(t, a):
        partner_real = other[n - 1 - t, 0]
        partner_imag = other[n - 1 - t, 1]
        x, off, f = scaled(a[0] - partner_real, a[1] - partner_imag)
        parts = split3(*f)
        f2 = complex_product(parts, parts)
        rows[t - half] = jnp.broadcast_to(diagonal(x, off, f, f2), (8, w))
        return x, f, parts, f2

    rates = jnp.where(side == 0, rates_ref[0:1, :], rates_ref[1:2, :])
    hist[0, 0] = jnp.zeros((w, w), f32)
    hist[0, 1] = jnp.where(eye, -0.5 * rates, 0.0)

    def first_half(t, carry):
        a = slab_at(t)
        at_hand = (a % 2) == side
        held = jnp.where(at_hand, a, n - 1 - a)

        @pl.when((held != me) & (held != aside))
        def _():
            arrived(o_buf, o_recv, held)

        o_forward(held).start()
        b = coupling_at(t)
        c = n - 2 - b

        @pl.when((t % 2) == side)
        def _():
            direct(c)
            m_forward(c).start()

            @pl.when(b != c)
            def _():
                direct(b)
                m_forward(b).start()

        @pl.when((t % 2) != side)
        def _():
            arrived(m_buf, m_recv, b)

        @pl.when(jnp.logical_not(at_hand))
        def _():
            arrived(o_buf, o_recv, a)

        s_forward(t).start()
        chain(t, matrix(t, t), t + 1)
        return carry

    lax.fori_loop(0, half, first_half, 0)

    def later_waits(t, coupled):
        a = slab_at(t)

        @pl.when((a % 2) != side)
        def _():
            arrived(o_buf, o_recv, a)

        if coupled:
            @pl.when((t % 2) != side)
            def _():
                arrived(m_buf, m_recv, coupling_at(t))

        s_forward(n - 1 - t).wait_recv()

    def row_copy(t):
        return remote(
            rows.at[t - half], rows_in.at[mine], r_send.at[t - half], r_recv.at[mine], slab_at(t)
        )

    def deliver(t):
        target = slab_at(t)

        @pl.when((target // group) == (me // group))
        def _():
            @pl.when(target == me)
            def _():
                rows_in[mine] = rows[t - half]

            @pl.when(target != me)
            def _():
                row_copy(t).start()

    def t_copy(k):
        return remote(
            crossing_own, crossing_in.at[mine], t_send.at[k - 1], t_recv.at[mine],
            base + (me - base + k) % group,
        )

    later_waits(half, half < n - 1)
    a = matrix(half, half)
    gamma_left = -2.0 * hist[half, 1]
    x, f, parts, f2 = final(half, a)
    gr, gi = completed(x, f, parts, f2)
    gamma_right = -2.0 * other[half - 1, 1]
    forward = product(split(gamma_left), split(jnp.concatenate([gr, gi], axis=1)))
    backward = product(split(jnp.concatenate([gr, gi], axis=0)), split(gamma_right))
    total = jnp.sum(forward[:, :w] * backward[:w] + forward[:, w:] * backward[w:])
    crossing_own[...] = jnp.full((8, 128), total, f32)
    chain(half, a, half)

    def last_half(t, carry):
        later_waits(t, True)
        deliver(t - 1)
        a = matrix(t, half)
        final(t, a)
        chain(t, a, half)
        return carry

    lax.fori_loop(half + 1, n - 1, last_half, 0)

    @pl.when(side == 0)
    def _():
        crossing_in[mine] = crossing_own[...]
        for k in range(1, group):
            t_copy(k).start()

    later_waits(n - 1, False)
    deliver(n - 2)
    final(n - 1, matrix(n - 1, half))
    deliver(n - 1)

    def row_wait(e):
        remote(rows.at[0], rows_in.at[e], r_send.at[0], r_recv.at[e], partner).wait_recv()

    sender_side = jnp.where(me < half, 1, 0)
    for e in range(ne):
        pl.when(base + 2 * e + sender_side != me)(functools.partial(row_wait, e))

    def t_wait(e):
        remote(crossing_own, crossing_in.at[e], t_send.at[0], t_recv.at[e], partner).wait_recv()

    for e in range(ne):
        pl.when(base + 2 * e != me)(functools.partial(t_wait, e))
    for e in range(ne):
        spectral_ref[0, e : e + 1, :] = rows_in[e, 0:1, :]
        crossing_ref[e] = crossing_in[e, 0, 0]

    def sent_first(j, k):
        o_part(j, k, partner).wait_send()
        used(j, lambda: top_part(j, k, partner).wait_send())

    def sent_second(j, k):
        used(j, lambda: bottom_part(j, k, partner).wait_send())

    for k in range(len(targets)):
        sent_first(me, k)
        sent_second(me, k)
    if square:
        sent_first(aside, 2)
        sent_second(above, 2)

    @pl.when(side == 0)
    def _():
        for k in range(1, group):
            t_copy(k).wait_send()

    def drain(t, carry):
        a = slab_at(t)
        o_forward(jnp.where((a % 2) == side, a, n - 1 - a)).wait_send()
        b = coupling_at(t)
        c = n - 2 - b

        @pl.when((t % 2) == side)
        def _():
            m_forward(c).wait_send()

            @pl.when(b != c)
            def _():
                m_forward(b).wait_send()

        s_forward(t).wait_send()
        target = slab_at(t + half)

        @pl.when(((target // group) == (me // group)) & (target != me))
        def _():
            row_copy(t + half).wait_send()

        return carry

    lax.fori_loop(0, half, drain, 0)


def solution(mesh):
    n = mesh.shape["slab"]

    def on_device(onsite, coupling, pattern, contact_rates, energy_index):
        w = onsite.shape[1]
        ne = energy_index.shape[0]
        half = n // 2
        dma = pltpu.SemaphoreType.DMA
        return pl.pallas_call(
            functools.partial(kernel, n, ne, w),
            out_shape=(
                jax.ShapeDtypeStruct((1, ne, w), f32),
                jax.ShapeDtypeStruct((ne,), f32),
            ),
            in_specs=[
                pl.BlockSpec(memory_space=pl.ANY),
                pl.BlockSpec(memory_space=pl.ANY),
                pl.BlockSpec(memory_space=pltpu.SMEM),
                pl.BlockSpec(memory_space=pltpu.VMEM),
                pl.BlockSpec(memory_space=pltpu.SMEM),
            ],
            out_specs=(
                pl.BlockSpec(memory_space=pltpu.VMEM),
                pl.BlockSpec(memory_space=pltpu.SMEM),
            ),
            scratch_shapes=[
                pltpu.VMEM((2, w, w), f32),
                pltpu.VMEM((n, w // 2 + 8, w), f32),
                pltpu.VMEM((n, w, w), f32),
                pltpu.VMEM((half + 1, 2, w, w), f32),
                pltpu.VMEM((half, 2, w, w), f32),
                pltpu.VMEM((2, 2, w, w), bf16),
                pltpu.VMEM((half, 8, w), f32),
                pltpu.VMEM((8, 128), f32),
                pltpu.VMEM((ne, 8, w), f32),
                pltpu.VMEM((ne, 8, 128), f32),
                dma((2,)), dma((half - 1,)), dma((half - 1,)), dma((half - 1,)), dma((n,)), dma((n,)), dma((n,)), dma((n,)), dma((n,)),
                dma((half,)), dma((half,)), dma((half,)), dma((ne,)), dma((2 * ne - 1,)), dma((ne,)),
            ],
            compiler_params=pltpu.CompilerParams(
                collective_id=0, has_side_effects=True, vmem_limit_bytes=60 * 2**20
            ),
        )(onsite, coupling, pattern, contact_rates, energy_index)

    return jax.shard_map(
        on_device,
        mesh=mesh,
        in_specs=(
            P("slab", None, None),
            P("slab", None, None),
            P("slab", None, None),
            P(),
            P("energy"),
        ),
        out_specs=(P("slab", "energy", None), P("energy")),
        check_vma=False,
    )
```

profile of v0, /device:TPU:0, one launch (start us, length us, event | category | flops | bytes accessed | tf_op | source)
XLA Modules:
  0.0 46.4 jit_solution(4756591079578819041)
XLA Ops:
  0.6 43.9 %shard_map.68 = (f32[1,4,256]{2,1,0:T(4,128)}, f32[4]{0:T(128)}) custom-call(f32[1,256,256]{2,1,0:T(8,128)} %onsite_in.1, f32[1,256,256]{2,1,0:T(8,128)} %coupling_in.1, s32[1,4,4]{2,1,0:T(4,128)} %pattern_ref.1, f32[2,256]{1,0:T(2,128)} %rates_ref.1, s32[4]{0:T(128)} %index_ref.1), custom_call_target="tpu_custom_call" | custom-call | tf_op jit(solution)/shard_map/pallas_call | solution.py:462
  44.6 0.0 copy-start
  44.6 1.3 %copy.9 = f32[1,4,256]{2,1,0:T(4,128)} copy(f32[1,4,256]{2,1,0:T(4,128)} %get-tuple-element.4) | data formatting | bytes 8192
  45.8 0.0 copy-done
  45.9 0.5 %copy.10 = f32[4]{0:T(128)} copy(f32[4]{0:T(128)S(1)} %copy-done) | data formatting | bytes 32
Async XLA Ops:
  44.6 1.3 %copy-start = (f32[4]{0:T(128)S(1)}, f32[4]{0:T(128)}, u32[]{:S(2)}) copy-start(f32[4]{0:T(128)} %get-tuple-element.5) | copy-start | bytes 52
where the time goes:
time: 46.6 us; the launch traced here: 46.4 us
  Pallas kernels  43.9 us (94%)
  local copies, waits for them, and re-layouts  1.78 us (4%)
  between operations  0.65 us (1%)
    pallas_call x1, Pallas kernels, on_device(): pl.pallas_call(functools.partial(kernel, n, ne, w), out_shape=(jax.ShapeD...  43.9 us
    unnamed x4, local copies, waits for them, and re-layouts  1.78 us

commit v1 on v0

v1 whole, which is shorter than its diff:
```python
import functools

import jax
import jax.numpy as jnp
from jax import lax
from jax.experimental import pallas as pl
from jax.experimental.pallas import tpu as pltpu
from jax.sharding import PartitionSpec as P

energy_floor = -0.2
energy_spacing = 0.0125
broadening = 0.3
MESH = pl.DeviceIdType.MESH
f32, bf16 = jnp.float32, jnp.bfloat16


def split(x):
    high = x.astype(bf16)
    return high, (x - high.astype(f32)).astype(bf16)


def product(left, right):
    return jnp.dot(
        jnp.concatenate([left[0], left[0], left[1]], axis=1),
        jnp.concatenate([right[0], right[1], right[0]], axis=0),
        preferred_element_type=f32,
    )


def complex_product(left, right):
    first = product(left[0], right[0])
    second = product(left[1], right[1])
    third = product(left[2], right[2])
    return first - second, third - first - second


def split3(real, imag):
    return split(real), split(imag), split(real + imag)


def exclusive(index, other, count):
    if count & (count - 1):
        return (index + other) % count
    total, bit = 0, 1
    while bit < count:
        total = total + (((index // bit) + (other // bit) % 2) % 2) * bit
        bit *= 2
    return total


def kernel(
    n, ne, w,
    onsite_in, coupling_in, pattern_ref, rates_ref, index_ref,
    spectral_ref, crossing_ref,
    raw, o_buf, m_buf, bare, hist, other, current, factor, rows, crossing_own, rows_in, crossing_in,
    local_sem, o_send, m_send, o_relay, m_relay, f_send, o_recv, m_recv,
    s_send, s_recv, r_send, r_recv, t_send, t_recv,
):
    half = n // 2
    group = 2 * ne
    me = lax.axis_index("slab")
    side = me % 2
    partner = me + 1 - 2 * side
    chip = me // 2
    mine = chip % ne
    base = (me // group) * group
    square = half == 4

    def slab_at(t):
        return t + side * (n - 1 - 2 * t)

    def coupling_at(t):
        return t + side * (n - 2 - 2 * t)

    def remote(src, dst, send, recv, target):
        return pltpu.make_async_remote_copy(
            src_ref=src, dst_ref=dst, send_sem=send, recv_sem=recv,
            device_id={"slab": target}, device_id_type=MESH,
        )

    own_o = pltpu.make_async_copy(onsite_in.at[0], raw.at[0], local_sem.at[0])
    own_m = pltpu.make_async_copy(coupling_in.at[0], raw.at[1], local_sem.at[1])
    own_o.start()
    own_m.start()

    barrier = pltpu.get_barrier_semaphore()
    for step in range(1, n):
        pl.semaphore_signal(
            barrier, inc=1, device_id={"slab": (me + step) % n}, device_id_type=MESH
        )

    h = w // 2
    tile_row = lax.broadcasted_iota(jnp.int32, (h, h), 0)
    tile_column = lax.broadcasted_iota(jnp.int32, (h, h), 1)

    def packed(block):
        last = block[h:, h:]
        o_buf[me, :h, :h] = jnp.where(tile_row >= tile_column, block[:h, :h], last)
        o_buf[me, :h, h:] = block[:h, h:]
        diag = jnp.sum(jnp.where(tile_row == tile_column, last, 0.0), axis=0, keepdims=True)
        o_buf[me, h:, :] = jnp.broadcast_to(jnp.concatenate([diag, diag], axis=1), (8, w))

    def unpacked(j):
        both = o_buf[j, :h, :h]
        corner = o_buf[j, :h, h:]
        turned = both.T
        first = jnp.where(tile_row >= tile_column, both, turned)
        last = jnp.where(tile_row < tile_column, both, turned)
        last = jnp.where(tile_row == tile_column, o_buf[j, h : h + 1, :h], last)
        return jnp.concatenate(
            [
                jnp.concatenate([first, corner], axis=1),
                jnp.concatenate([corner.T, last], axis=1),
            ],
            axis=0,
        )

    own_o.wait()
    own_m.wait()
    packed(raw[0])
    tiles = pattern_ref.shape[1]
    size = w // tiles
    lane_tile = lax.broadcasted_iota(jnp.int32, (1, w), 1) // size
    for p in range(tiles):
        kept = jnp.zeros((1, w), f32)
        for q in range(tiles):
            kept = jnp.where(lane_tile == q, pattern_ref[0, p, q].astype(f32), kept)
        m_buf[me, p * size : (p + 1) * size, :] = raw[1, p * size : (p + 1) * size, :] * kept
    pl.semaphore_wait(barrier, n - 1)

    o_rows = o_buf.shape[1]
    o_cut = (o_rows // 16 + 1) * 8
    o_part = (pl.ds(0, o_cut), pl.ds(o_cut, o_rows - o_cut))
    m_part = (pl.ds(0, h), pl.ds(h, w - h))
    user = jnp.where(me < half, 0, 1)
    o_step = jnp.where(me < half, me, n - 1 - me)
    m_step = jnp.where(me < half, me, n - 2 - me)
    spread = (1, 2) if square else tuple(range(1, half))

    def stage(step):
        if not square:
            return jnp.zeros_like(step)
        return jnp.where(step < 2, step, step - 1)

    def o_copy(j, p, send, target):
        view = o_buf.at[j, o_part[p]]
        return remote(view, view, send, o_recv.at[j, p], target)

    def m_copy(j, p, send, target):
        view = m_buf.at[j, m_part[p]]
        return remote(view, view, send, m_recv.at[j, p], target)

    def own_copies(copy, send, act):
        for order in (0, 1):
            for k in spread:
                p = order if k == 1 else 1 - order
                act(copy(me, p, send.at[k, p], exclusive(chip, k, half) * 2 + user))

    def partner_copies(copy, send, act):
        @pl.when(side != user)
        def _():
            for p in (0, 1):
                act(copy(me, p, send.at[0, p], partner))

    def start(c):
        c.start()

    def finish(c):
        c.wait_send()

    def own_stage(s):
        pl.when(stage(o_step) == s)(lambda: own_copies(o_copy, o_send, start))
        pl.when((stage(m_step) == s) & (me < n - 1))(lambda: own_copies(m_copy, m_send, start))

    own_stage(0)
    partner_copies(o_copy, o_send, start)
    pl.when(me < n - 1)(lambda: partner_copies(m_copy, m_send, start))

    def passes(j, p):
        return chip == exclusive(j // 2, p + 1, half)

    def o_relayed(t, p):
        j = slab_at(t)
        return o_copy(j, p, o_relay.at[t], exclusive(chip, 2 - p, half) * 2 + side)

    def m_relayed(t, p):
        j = coupling_at(t)
        return m_copy(j, p, m_relay.at[t], exclusive(chip, 2 - p, half) * 2 + side)

    def m_shared(t):
        return (side == 1) & (t == half - 1)

    def relay_o(t):
        if square:
            for p in (0, 1):

                @pl.when(passes(slab_at(t), p))
                def _():
                    o_copy(slab_at(t), p, o_relay.at[t], partner).wait_recv()
                    o_relayed(t, p).start()

    def rest_o(t):
        j = slab_at(t)
        for p in (0, 1):
            waits = j != me
            if square:
                waits = waits & jnp.logical_not(passes(j, p))
            pl.when(waits)(lambda p=p: o_copy(j, p, o_relay.at[t], partner).wait_recv())

    def relay_m(t):
        if square:
            for p in (0, 1):

                @pl.when(passes(coupling_at(t), p) & jnp.logical_not(m_shared(t)))
                def _():
                    m_copy(coupling_at(t), p, m_relay.at[t], partner).wait_recv()
                    m_relayed(t, p).start()

    def handed(p):
        return m_copy(half - 1, p, f_send.at[p], partner)

    hands = (side == 0) & (partner != half - 1)

    def rest_m(t):
        j = coupling_at(t)
        for p in (0, 1):
            waits = j != me
            if square:
                waits = waits & (jnp.logical_not(passes(j, p)) | m_shared(t))
            pl.when(waits)(lambda p=p: m_copy(j, p, m_relay.at[t], partner).wait_recv())

        @pl.when(hands & (t == half - 1))
        def _():
            for p in (0, 1):
                handed(p).start()

    row_at = lax.broadcasted_iota(jnp.int32, (w, w), 0)
    column_at = lax.broadcasted_iota(jnp.int32, (w, w), 1)
    eye = row_at == column_at
    energy = energy_floor + energy_spacing * index_ref[mine].astype(f32)

    def scaled(real, imag):
        diag_real = jnp.sum(jnp.where(eye, real, 0.0), axis=0, keepdims=True)
        diag_imag = jnp.sum(jnp.where(eye, imag, 0.0), axis=0, keepdims=True)
        modulus = diag_real * diag_real + diag_imag * diag_imag
        xr = diag_real / modulus
        xi = -diag_imag / modulus
        xrc = jnp.sum(jnp.where(eye, xr, 0.0), axis=1, keepdims=True)
        xic = jnp.sum(jnp.where(eye, xi, 0.0), axis=1, keepdims=True)
        off_real = jnp.where(eye, 0.0, real)
        off_imag = jnp.where(eye, 0.0, imag)
        fr = off_real * xr - off_imag * xi
        fi = off_real * xi + off_imag * xr
        return (xr, xi, xrc, xic), (off_real, off_imag), (fr, fi)

    def completed(x, f, f_parts, f2):
        third = complex_product(f_parts, split3(*f2))
        hr = jnp.where(eye, 1.0, 0.0) - f[0] + f2[0] - third[0]
        hi = f2[1] - f[1] - third[1]
        xrc, xic = x[2], x[3]
        return xrc * hr - xic * hi, xrc * hi + xic * hr

    def diagonal(x, off, f, f2):
        xr, xi, xrc, xic = x
        zr = off[0] * xrc - off[1] * xic
        zi = off[0] * xic + off[1] * xrc
        wr = f[0] - f2[0]
        wi = f[1] - f2[1]
        dr = 1.0 + jnp.sum(zr * wr - zi * wi, axis=0, keepdims=True)
        di = jnp.sum(zr * wi + zi * wr, axis=0, keepdims=True)
        return -2.0 * (xr * di + xi * dr)

    def keep_factor(t):
        m = m_buf[coupling_at(t)]
        high, low = split(m)
        factor[t, side, 0] = high
        factor[t, side, 1] = low
        high, low = split(m.T)
        factor[t, 1 - side, 0] = high
        factor[t, 1 - side, 1] = low

    def inverted(a):
        x, off, f = scaled(*a)
        parts = split3(*f)
        f2 = complex_product(parts, parts)
        return completed(x, f, parts, f2)

    def stepped(g, first, second, out):
        gs = split(jnp.concatenate(g, axis=0))
        u = product(gs, (first[0], first[1]))
        us = split(jnp.concatenate([u[:w], u[w:]], axis=1))
        s = product((second[0], second[1]), us)
        out[0] = s[:, :w]
        out[1] = s[:, w:]

    def final(k, real, imag):
        x, off, f = scaled(real, imag)
        parts = split3(*f)
        f2 = complex_product(parts, parts)
        rows[k] = jnp.broadcast_to(diagonal(x, off, f, f2), (8, w))
        return x, f, parts, f2

    rates = jnp.where(side == 0, rates_ref[0:1, :], rates_ref[1:2, :])
    hist[0, 0] = jnp.zeros((w, w), f32)
    hist[0, 1] = jnp.where(eye, -0.5 * rates, 0.0)
    widths = jnp.where(eye, broadening, 0.0)

    relay_o(0)

    def outward(t, carry):
        rest_o(t)
        relay_m(t)
        own_stage(t + 1)
        level = jnp.where(eye, energy, 0.0) - unpacked(slab_at(t))
        bare[t] = level
        g = inverted((level - hist[t, 0], widths - hist[t, 1]))
        rest_m(t)
        pl.when(t < half - 1)(lambda: relay_o(jnp.minimum(t + 1, half - 1)))
        keep_factor(t)
        stepped(g, factor.at[t, 0], factor.at[t, 1], hist.at[t + 1])
        return carry

    lax.fori_loop(0, half, outward, 0)

    swap = remote(hist.at[half], other, s_send.at[0], s_recv.at[0], partner)
    swap.start()

    def row_copy(k):
        return remote(
            rows.at[k], rows_in.at[mine], r_send.at[k], r_recv.at[mine], slab_at(half - 1 - k)
        )

    def deliver(k):
        target = slab_at(half - 1 - k)

        @pl.when((target // group) == (me // group))
        def _():
            @pl.when(target == me)
            def _():
                rows_in[mine] = rows[k]

            @pl.when(target != me)
            def _():
                row_copy(k).start()

    def t_copy(k):
        return remote(
            crossing_own, crossing_in.at[mine], t_send.at[k - 1], t_recv.at[mine],
            base + (me - base + k) % group,
        )

    def behind(t, g):
        stepped(g, factor.at[t, 1], factor.at[t, 0], current)

    last = half - 1
    swap.wait_recv()
    real = bare[last] - other[0]
    imag = widths - other[1]
    x, f, parts, f2 = final(0, real - hist[last, 0], imag - hist[last, 1])

    @pl.when(side == 1)
    def _():
        gr, gi = completed(x, f, parts, f2)
        gamma_left = -2.0 * other[1]
        gamma_right = -2.0 * hist[last, 1]
        forward = product(split(gamma_left), split(jnp.concatenate([gr, gi], axis=1)))
        backward = product(split(jnp.concatenate([gr, gi], axis=0)), split(gamma_right))
        total = jnp.sum(forward[:, :w] * backward[:w] + forward[:, w:] * backward[w:])
        crossing_own[...] = jnp.full((8, 128), total, f32)

    behind(last - 1, inverted((real, imag)))

    def inward(k, carry):
        deliver(k - 1)
        t = last - k
        real = bare[t] - current[0]
        imag = widths - current[1]
        final(k, real - hist[t, 0], imag - hist[t, 1])
        behind(t - 1, inverted((real, imag)))
        return carry

    lax.fori_loop(1, last, inward, 0)

    @pl.when(side == 1)
    def _():
        crossing_in[mine] = crossing_own[...]
        for k in range(1, group):
            t_copy(k).start()

    deliver(last - 1)
    final(last, bare[0] - current[0] - hist[0, 0], widths - current[1] - hist[0, 1])
    deliver(last)

    def row_wait(e):
        remote(rows.at[0], rows_in.at[e], r_send.at[0], r_recv.at[e], partner).wait_recv()

    for e in range(ne):
        pl.when(base + 2 * e + user != me)(functools.partial(row_wait, e))

    def t_wait(e):
        remote(crossing_own, crossing_in.at[e], t_send.at[0], t_recv.at[e], partner).wait_recv()

    for e in range(ne):
        pl.when(base + 2 * e + 1 != me)(functools.partial(t_wait, e))
    for e in range(ne):
        spectral_ref[0, e : e + 1, :] = rows_in[e, 0:1, :]
        crossing_ref[e] = crossing_in[e, 0, 0]

    own_copies(o_copy, o_send, finish)
    partner_copies(o_copy, o_send, finish)

    @pl.when(me < n - 1)
    def _():
        own_copies(m_copy, m_send, finish)
        partner_copies(m_copy, m_send, finish)

    @pl.when(hands)
    def _():
        for p in (0, 1):
            handed(p).wait_send()

    swap.wait_send()

    @pl.when(side == 1)
    def _():
        for k in range(1, group):
            t_copy(k).wait_send()

    def drain(t, carry):
        if square:
            for p in (0, 1):
                pl.when(passes(slab_at(t), p))(lambda p=p: o_relayed(t, p).wait_send())
                pl.when(passes(coupling_at(t), p) & jnp.logical_not(m_shared(t)))(
                    lambda p=p: m_relayed(t, p).wait_send()
                )
        target = slab_at(half - 1 - t)

        @pl.when(((target // group) == (me // group)) & (target != me))
        def _():
            row_copy(t).wait_send()

        return carry

    lax.fori_loop(0, half, drain, 0)


def solution(mesh):
    n = mesh.shape["slab"]

    def on_device(onsite, coupling, pattern, contact_rates, energy_index):
        w = onsite.shape[1]
        ne = energy_index.shape[0]
        half = n // 2
        dma = pltpu.SemaphoreType.DMA
        return pl.pallas_call(
            functools.partial(kernel, n, ne, w),
            out_shape=(
                jax.ShapeDtypeStruct((1, ne, w), f32),
                jax.ShapeDtypeStruct((ne,), f32),
            ),
            in_specs=[
                pl.BlockSpec(memory_space=pl.ANY),
                pl.BlockSpec(memory_space=pl.ANY),
                pl.BlockSpec(memory_space=pltpu.SMEM),
                pl.BlockSpec(memory_space=pltpu.VMEM),
                pl.BlockSpec(memory_space=pltpu.SMEM),
            ],
            out_specs=(
                pl.BlockSpec(memory_space=pltpu.VMEM),
                pl.BlockSpec(memory_space=pltpu.SMEM),
            ),
            scratch_shapes=[
                pltpu.VMEM((2, w, w), f32),
                pltpu.VMEM((n, w // 2 + 8, w), f32),
                pltpu.VMEM((n, w, w), f32),
                pltpu.VMEM((half, w, w), f32),
                pltpu.VMEM((half + 1, 2, w, w), f32),
                pltpu.VMEM((2, w, w), f32),
                pltpu.VMEM((2, w, w), f32),
                pltpu.VMEM((half, 2, 2, w, w), bf16),
                pltpu.VMEM((half, 8, w), f32),
                pltpu.VMEM((8, 128), f32),
                pltpu.VMEM((ne, 8, w), f32),
                pltpu.VMEM((ne, 8, 128), f32),
                dma((2,)), dma((half, 2)), dma((half, 2)), dma((half,)), dma((half,)), dma((2,)), dma((n, 2)), dma((n, 2)),
                dma((1,)), dma((1,)), dma((half,)), dma((ne,)), dma((2 * ne - 1,)), dma((ne,)),
            ],
            compiler_params=pltpu.CompilerParams(
                collective_id=0, has_side_effects=True, vmem_limit_bytes=60 * 2**20
            ),
        )(onsite, coupling, pattern, contact_rates, energy_index)

    return jax.shard_map(
        on_device,
        mesh=mesh,
        in_specs=(
            P("slab", None, None),
            P("slab", None, None),
            P("slab", None, None),
            P(),
            P("energy"),
        ),
        out_specs=(P("slab", "energy", None), P("energy")),
        check_vma=False,
    )
```

time: 46.6 us -> 50.1 us (1.075)
  Pallas kernels: 43.9 us -> 47.5 us
    pallas_call x1, Pallas kernels: 43.9 us -> 47.5 us  [on_device(): pl.pallas_call(functools.partial(kernel, n, ne, w), out_shape=(jax.ShapeD...]
where the time goes in v1:
time: 50.1 us; the launch traced here: 49.9 us
  Pallas kernels  47.5 us (95%)
  local copies, waits for them, and re-layouts  1.78 us (4%)
  between operations  0.65 us (1%)
    pallas_call x1, Pallas kernels, on_device(): pl.pallas_call(functools.partial(kernel, n, ne, w), out_shape=(jax.ShapeD...  47.5 us
    unnamed x4, local copies, waits for them, and re-layouts  1.78 us

profile of v1, /device:TPU:0, one launch (start us, length us, event | category | flops | bytes accessed | tf_op | source)
XLA Modules:
  0.0 49.9 jit_solution(15743825330766217092)
XLA Ops:
  0.6 47.5 %shard_map.68 = (f32[1,4,256]{2,1,0:T(4,128)}, f32[4]{0:T(128)}) custom-call(f32[1,256,256]{2,1,0:T(8,128)} %onsite_in.1, f32[1,256,256]{2,1,0:T(8,128)} %coupling_in.1, s32[1,4,4]{2,1,0:T(4,128)} %pattern_ref.1, f32[2,256]{1,0:T(2,128)} %rates_ref.1, s32[4]{0:T(128)} %index_ref.1), custom_call_target="tpu_custom_call" | custom-call | tf_op jit(solution)/shard_map/pallas_call | solution.py:455
  48.1 0.0 copy-start
  48.2 1.3 %copy.9 = f32[1,4,256]{2,1,0:T(4,128)} copy(f32[1,4,256]{2,1,0:T(4,128)} %get-tuple-element.4) | data formatting | bytes 8192
  49.4 0.0 copy-done
  49.4 0.5 %copy.10 = f32[4]{0:T(128)} copy(f32[4]{0:T(128)S(1)} %copy-done) | data formatting | bytes 32
Async XLA Ops:
  48.1 1.3 %copy-start = (f32[4]{0:T(128)S(1)}, f32[4]{0:T(128)}, u32[]{:S(2)}) copy-start(f32[4]{0:T(128)} %get-tuple-element.5) | copy-start | bytes 52

commit v2 on v0

--- a/solution.py
+++ b/solution.py
@@ -27,15 +27,21 @@
     )
 
 
+def rounded(real, imag):
+    return jnp.concatenate([real.astype(bf16), imag.astype(bf16)], axis=1)
+
+
+def doubled(real, imag):
+    real, imag = real.astype(bf16), imag.astype(bf16)
+    return jnp.concatenate(
+        [jnp.concatenate([real, imag], axis=1), jnp.concatenate([-imag, real], axis=1)], axis=0
+    )
+
+
 def complex_product(left, right):
-    first = product(left[0], right[0])
-    second = product(left[1], right[1])
-    third = product(left[2], right[2])
-    return first - second, third - first - second
-
-
-def split3(real, imag):
-    return split(real), split(imag), split(real + imag)
+    both = jnp.dot(left, doubled(*right), preferred_element_type=f32)
+    width = both.shape[1] // 2
+    return both[:, :width], both[:, width:]
 
 
 def exclusive(index, other, count):
@@ -227,8 +233,8 @@
         fi = off_real * xi + off_imag * xr
         return (xr, xi, xrc, xic), (off_real, off_imag), (fr, fi)
 
-    def completed(x, f, f_parts, f2):
-        third = complex_product(f_parts, split3(*f2))
+    def completed(x, f, left, f2):
+        third = complex_product(left, f2)
         hr = jnp.where(eye, 1.0, 0.0) - f[0] + f2[0] - third[0]
         hi = f2[1] - f[1] - third[1]
         xrc, xic = x[2], x[3]
@@ -259,9 +265,9 @@
         factor[1 - side, 0] = high
         factor[1 - side, 1] = low
         x, off, f = scaled(*a)
-        parts = split3(*f)
-        f2 = complex_product(parts, parts)
-        g = completed(x, f, parts, f2)
+        left = rounded(*f)
+        f2 = complex_product(left, f)
+        g = completed(x, f, left, f2)
         gs = split(jnp.concatenate(g, axis=0))
         u = product(gs, (factor[0, 0], factor[0, 1]))
         us = split(jnp.concatenate([u[:w], u[w:]], axis=1))
@@ -273,10 +279,10 @@
         partner_real = other[n - 1 - t, 0]
         partner_imag = other[n - 1 - t, 1]
         x, off, f = scaled(a[0] - partner_real, a[1] - partner_imag)
-        parts = split3(*f)
-        f2 = complex_product(parts, parts)
+        left = rounded(*f)
+        f2 = complex_product(left, f)
         rows[t - half] = jnp.broadcast_to(diagonal(x, off, f, f2), (8, w))
-        return x, f, parts, f2
+        return x, f, left, f2
 
     rates = jnp.where(side == 0, rates_ref[0:1, :], rates_ref[1:2, :])
     hist[0, 0] = jnp.zeros((w, w), f32)
@@ -360,8 +366,8 @@
     later_waits(half, half < n - 1)
     a = matrix(half, half)
     gamma_left = -2.0 * hist[half, 1]
-    x, f, parts, f2 = final(half, a)
-    gr, gi = completed(x, f, parts, f2)
+    x, f, left, f2 = final(half, a)
+    gr, gi = completed(x, f, left, f2)
     gamma_right = -2.0 * other[half - 1, 1]
     forward = product(split(gamma_left), split(jnp.concatenate([gr, gi], axis=1)))
     backward = product(split(jnp.concatenate([gr, gi], axis=0)), split(gamma_right))

time: 46.6 us -> 43.1 us (0.925)
  Pallas kernels: 43.9 us -> 40.5 us
    pallas_call x1, Pallas kernels: 43.9 us -> 40.5 us  [on_device(): pl.pallas_call(functools.partial(kernel, n, ne, w), out_shape=(jax.ShapeD...]
where the time goes in v2:
time: 43.1 us; the launch traced here: 43 us
  Pallas kernels  40.5 us (94%)
  local copies, waits for them, and re-layouts  1.78 us (4%)
  between operations  0.65 us (2%)
    pallas_call x1, Pallas kernels, on_device(): pl.pallas_call(functools.partial(kernel, n, ne, w), out_shape=(jax.ShapeD...  40.5 us
    unnamed x4, local copies, waits for them, and re-layouts  1.78 us

profile of v2, /device:TPU:0, one launch (start us, length us, event | category | flops | bytes accessed | tf_op | source)
XLA Modules:
  0.0 43.0 jit_solution(16880814952749275523)
XLA Ops:
  0.6 40.5 %shard_map.68 = (f32[1,4,256]{2,1,0:T(4,128)}, f32[4]{0:T(128)}) custom-call(f32[1,256,256]{2,1,0:T(8,128)} %onsite_in.1, f32[1,256,256]{2,1,0:T(8,128)} %coupling_in.1, s32[1,4,4]{2,1,0:T(4,128)} %pattern_ref.1, f32[2,256]{1,0:T(2,128)} %rates_ref.1, s32[4]{0:T(128)} %index_ref.1), custom_call_target="tpu_custom_call" | custom-call | tf_op jit(solution)/shard_map/pallas_call | solution.py:468
  41.2 0.0 copy-start
  41.2 1.3 %copy.9 = f32[1,4,256]{2,1,0:T(4,128)} copy(f32[1,4,256]{2,1,0:T(4,128)} %get-tuple-element.4) | data formatting | bytes 8192
  42.4 0.0 copy-done
  42.4 0.5 %copy.10 = f32[4]{0:T(128)} copy(f32[4]{0:T(128)S(1)} %copy-done) | data formatting | bytes 32
Async XLA Ops:
  41.2 1.3 %copy-start = (f32[4]{0:T(128)S(1)}, f32[4]{0:T(128)}, u32[]{:S(2)}) copy-start(f32[4]{0:T(128)} %get-tuple-element.5) | copy-start | bytes 52

commit v3 on v1

--- a/solution.py
+++ b/solution.py
@@ -27,15 +27,21 @@
     )
 
 
+def rounded(real, imag):
+    return jnp.concatenate([real.astype(bf16), imag.astype(bf16)], axis=1)
+
+
+def doubled(real, imag):
+    real, imag = real.astype(bf16), imag.astype(bf16)
+    return jnp.concatenate(
+        [jnp.concatenate([real, imag], axis=1), jnp.concatenate([-imag, real], axis=1)], axis=0
+    )
+
+
 def complex_product(left, right):
-    first = product(left[0], right[0])
-    second = product(left[1], right[1])
-    third = product(left[2], right[2])
-    return first - second, third - first - second
-
-
-def split3(real, imag):
-    return split(real), split(imag), split(real + imag)
+    both = jnp.dot(left, doubled(*right), preferred_element_type=f32)
+    width = both.shape[1] // 2
+    return both[:, :width], both[:, width:]
 
 
 def exclusive(index, other, count):
@@ -140,7 +146,7 @@
     def stage(step):
         if not square:
             return jnp.zeros_like(step)
-        return jnp.where(step < 2, step, step - 1)
+        return jnp.zeros_like(step)
 
     def o_copy(j, p, send, target):
         view = o_buf.at[j, o_part[p]]
@@ -253,8 +259,8 @@
         fi = off_real * xi + off_imag * xr
         return (xr, xi, xrc, xic), (off_real, off_imag), (fr, fi)
 
-    def completed(x, f, f_parts, f2):
-        third = complex_product(f_parts, split3(*f2))
+    def completed(x, f, left, f2):
+        third = complex_product(left, f2)
         hr = jnp.where(eye, 1.0, 0.0) - f[0] + f2[0] - third[0]
         hi = f2[1] - f[1] - third[1]
         xrc, xic = x[2], x[3]
@@ -281,9 +287,9 @@
 
     def inverted(a):
         x, off, f = scaled(*a)
-        parts = split3(*f)
-        f2 = complex_product(parts, parts)
-        return completed(x, f, parts, f2)
+        left = rounded(*f)
+        f2 = complex_product(left, f)
+        return completed(x, f, left, f2)
 
     def stepped(g, first, second, out):
         gs = split(jnp.concatenate(g, axis=0))
@@ -295,27 +301,27 @@
 
     def final(k, real, imag):
         x, off, f = scaled(real, imag)
-        parts = split3(*f)
-        f2 = complex_product(parts, parts)
+        left = rounded(*f)
+        f2 = complex_product(left, f)
         rows[k] = jnp.broadcast_to(diagonal(x, off, f, f2), (8, w))
-        return x, f, parts, f2
+        return x, f, left, f2
 
     rates = jnp.where(side == 0, rates_ref[0:1, :], rates_ref[1:2, :])
     hist[0, 0] = jnp.zeros((w, w), f32)
     hist[0, 1] = jnp.where(eye, -0.5 * rates, 0.0)
     widths = jnp.where(eye, broadening, 0.0)
 
-    relay_o(0)
+    if square:
+        for t in range(half):
+            relay_o(t)
+            relay_m(t)
 
     def outward(t, carry):
         rest_o(t)
-        relay_m(t)
-        own_stage(t + 1)
         level = jnp.where(eye, energy, 0.0) - unpacked(slab_at(t))
         bare[t] = level
         g = inverted((level - hist[t, 0], widths - hist[t, 1]))
         rest_m(t)
-        pl.when(t < half - 1)(lambda: relay_o(jnp.minimum(t + 1, half - 1)))
         keep_factor(t)
         stepped(g, factor.at[t, 0], factor.at[t, 1], hist.at[t + 1])
         return carry
@@ -356,11 +362,11 @@
     swap.wait_recv()
     real = bare[last] - other[0]
     imag = widths - other[1]
-    x, f, parts, f2 = final(0, real - hist[last, 0], imag - hist[last, 1])
+    x, f, left, f2 = final(0, real - hist[last, 0], imag - hist[last, 1])
 
     @pl.when(side == 1)
     def _():
-        gr, gi = completed(x, f, parts, f2)
+        gr, gi = completed(x, f, left, f2)
         gamma_left = -2.0 * other[1]
         gamma_right = -2.0 * hist[last, 1]
         forward = product(split(gamma_left), split(jnp.concatenate([gr, gi], axis=1)))

time: 50.1 us -> 41.2 us (0.82)
  Pallas kernels: 47.5 us -> 38.6 us
    pallas_call x1, Pallas kernels: 47.5 us -> 38.6 us  [on_device(): pl.pallas_call(functools.partial(kernel, n, ne, w), out_shape=(jax.ShapeD...]
where the time goes in v3:
time: 41.2 us; the launch traced here: 41 us
  Pallas kernels  38.6 us (94%)
  local copies, waits for them, and re-layouts  1.78 us (4%)
  between operations  0.65 us (2%)
    pallas_call x1, Pallas kernels, on_device(): pl.pallas_call(functools.partial(kernel, n, ne, w), out_shape=(jax.ShapeD...  38.6 us
    unnamed x4, local copies, waits for them, and re-layouts  1.78 us

profile of v3, /device:TPU:0, one launch (start us, length us, event | category | flops | bytes accessed | tf_op | source)
XLA Modules:
  0.0 41.0 jit_solution(10342123007090249741)
XLA Ops:
  0.6 38.6 %shard_map.68 = (f32[1,4,256]{2,1,0:T(4,128)}, f32[4]{0:T(128)}) custom-call(f32[1,256,256]{2,1,0:T(8,128)} %onsite_in.1, f32[1,256,256]{2,1,0:T(8,128)} %coupling_in.1, s32[1,4,4]{2,1,0:T(4,128)} %pattern_ref.1, f32[2,256]{1,0:T(2,128)} %rates_ref.1, s32[4]{0:T(128)} %index_ref.1), custom_call_target="tpu_custom_call" | custom-call | tf_op jit(solution)/shard_map/pallas_call | solution.py:461
  39.3 0.0 copy-start
  39.3 1.3 %copy.9 = f32[1,4,256]{2,1,0:T(4,128)} copy(f32[1,4,256]{2,1,0:T(4,128)} %get-tuple-element.4) | data formatting | bytes 8192
  40.5 0.0 copy-done
  40.5 0.5 %copy.10 = f32[4]{0:T(128)} copy(f32[4]{0:T(128)S(1)} %copy-done) | data formatting | bytes 32
Async XLA Ops:
  39.3 1.3 %copy-start = (f32[4]{0:T(128)S(1)}, f32[4]{0:T(128)}, u32[]{:S(2)}) copy-start(f32[4]{0:T(128)} %get-tuple-element.5) | copy-start | bytes 52

commit v4 on v3

--- a/solution.py
+++ b/solution.py
@@ -139,14 +139,7 @@
     o_part = (pl.ds(0, o_cut), pl.ds(o_cut, o_rows - o_cut))
     m_part = (pl.ds(0, h), pl.ds(h, w - h))
     user = jnp.where(me < half, 0, 1)
-    o_step = jnp.where(me < half, me, n - 1 - me)
-    m_step = jnp.where(me < half, me, n - 2 - me)
     spread = (1, 2) if square else tuple(range(1, half))
-
-    def stage(step):
-        if not square:
-            return jnp.zeros_like(step)
-        return jnp.zeros_like(step)
 
     def o_copy(j, p, send, target):
         view = o_buf.at[j, o_part[p]]
@@ -156,8 +149,8 @@
         view = m_buf.at[j, m_part[p]]
         return remote(view, view, send, m_recv.at[j, p], target)
 
-    def own_copies(copy, send, act):
-        for order in (0, 1):
+    def own_copies(copy, send, act, orders=(0, 1)):
+        for order in orders:
             for k in spread:
                 p = order if k == 1 else 1 - order
                 act(copy(me, p, send.at[k, p], exclusive(chip, k, half) * 2 + user))
@@ -174,11 +167,16 @@
     def finish(c):
         c.wait_send()
 
-    def own_stage(s):
-        pl.when(stage(o_step) == s)(lambda: own_copies(o_copy, o_send, start))
-        pl.when((stage(m_step) == s) & (me < n - 1))(lambda: own_copies(m_copy, m_send, start))
-
-    own_stage(0)
+    def send(order):
+        own_copies(o_copy, o_send, start, (order,))
+        pl.when(me < n - 1)(lambda: own_copies(m_copy, m_send, start, (order,)))
+
+    passing = (chip != 0) & (chip != half - 1)
+    send(0)
+    if square:
+        pl.when(jnp.logical_not(passing))(lambda: send(1))
+    else:
+        send(1)
     partner_copies(o_copy, o_send, start)
     pl.when(me < n - 1)(lambda: partner_copies(m_copy, m_send, start))
 
@@ -315,6 +313,7 @@
         for t in range(half):
             relay_o(t)
             relay_m(t)
+        pl.when(passing)(lambda: send(1))
 
     def outward(t, carry):
         rest_o(t)

time: 41.2 us -> 40.1 us (0.973)
  Pallas kernels: 38.6 us -> 37.5 us
    pallas_call x1, Pallas kernels: 38.6 us -> 37.5 us  [on_device(): pl.pallas_call(functools.partial(kernel, n, ne, w), out_shape=(jax.ShapeD...]
where the time goes in v4:
time: 40.1 us; the launch traced here: 39.9 us
  Pallas kernels  37.5 us (94%)
  local copies, waits for them, and re-layouts  1.78 us (4%)
  between operations  0.65 us (2%)
    pallas_call x1, Pallas kernels, on_device(): pl.pallas_call(functools.partial(kernel, n, ne, w), out_shape=(jax.ShapeD...  37.5 us
    unnamed x4, local copies, waits for them, and re-layouts  1.78 us

profile of v4, /device:TPU:0, one launch (start us, length us, event | category | flops | bytes accessed | tf_op | source)
XLA Modules:
  0.0 39.9 jit_solution(3515639014355580904)
XLA Ops:
  0.6 37.5 %shard_map.68 = (f32[1,4,256]{2,1,0:T(4,128)}, f32[4]{0:T(128)}) custom-call(f32[1,256,256]{2,1,0:T(8,128)} %onsite_in.1, f32[1,256,256]{2,1,0:T(8,128)} %coupling_in.1, s32[1,4,4]{2,1,0:T(4,128)} %pattern_ref.1, f32[2,256]{1,0:T(2,128)} %rates_ref.1, s32[4]{0:T(128)} %index_ref.1), custom_call_target="tpu_custom_call" | custom-call | tf_op jit(solution)/shard_map/pallas_call | solution.py:460
  38.1 0.0 copy-start
  38.1 1.3 %copy.9 = f32[1,4,256]{2,1,0:T(4,128)} copy(f32[1,4,256]{2,1,0:T(4,128)} %get-tuple-element.4) | data formatting | bytes 8192
  39.4 0.0 copy-done
  39.4 0.5 %copy.10 = f32[4]{0:T(128)} copy(f32[4]{0:T(128)S(1)} %copy-done) | data formatting | bytes 32
Async XLA Ops:
  38.1 1.3 %copy-start = (f32[4]{0:T(128)S(1)}, f32[4]{0:T(128)}, u32[]{:S(2)}) copy-start(f32[4]{0:T(128)} %get-tuple-element.5) | copy-start | bytes 52
